TPU v7x, 32 devices: a whole 2x2x4 slice. The times are simulated.
32 devices in a mesh: fsdp: 16 (over z, y, core), dp: 2 (over x).
Axes of the slice: x: 2, y: 2, z: 4, core: 2. Of those that a mesh axis runs over, the one named last changes fastest.
Arguments:
- tokens: bfloat16 [32, 256, 1152], P(('fsdp', 'dp')), may hold values from -12 to 12, as said below
- cond: bfloat16 [32, 1152], P(('fsdp', 'dp')), may hold values from -6 to 6
- segment_ids: int32 [32, 256], P(('fsdp', 'dp')), may hold values from 0 to 7, as said below
- ada_weight: bfloat16 [1152, 6912], P('fsdp'), may hold values from -0.1875 to 0.1875
- ada_bias: bfloat16 [6912], P('fsdp'), may hold values from -1 to 1
- qkv_weight: bfloat16 [1152, 3456], P('fsdp'), may hold values from -0.1875 to 0.1875
- qv_bias: bfloat16 [2304], P('fsdp'), may hold values from -1 to 1
- proj_weight: bfloat16 [1152, 1152], P('fsdp'), may hold values from -0.75 to 0.75
- proj_bias: bfloat16 [1152], P('fsdp'), may hold values from -1 to 1
- fc1_weight: bfloat16 [1152, 4608], P('fsdp'), may hold values from -0.1875 to 0.1875
- fc1_bias: bfloat16 [4608], P('fsdp'), may hold values from -1 to 1
- fc2_weight: bfloat16 [4608, 1152], P('fsdp'), may hold values from -0.09375 to 0.09375
- fc2_bias: bfloat16 [1152], P('fsdp'), may hold values from -1 to 1
- out_grad: bfloat16 [32, 256, 1152], P(('fsdp', 'dp')), may hold values from -6 to 6
Outputs:
- output: bfloat16 [32, 256, 1152], P(('fsdp', 'dp'))
- tokens_grad: bfloat16 [32, 256, 1152], P(('fsdp', 'dp'))
- ada_weight_grad: float32 [1152, 6912], P('fsdp')
- ada_bias_grad: float32 [6912], P('fsdp')
- qkv_weight_grad: float32 [1152, 3456], P('fsdp')
- qv_bias_grad: float32 [2304], P('fsdp')
- proj_weight_grad: float32 [1152, 1152], P('fsdp')
- proj_bias_grad: float32 [1152], P('fsdp')
- fc1_weight_grad: float32 [1152, 4608], P('fsdp')
- fc1_bias_grad: float32 [4608], P('fsdp')
- fc2_weight_grad: float32 [4608, 1152], P('fsdp')
- fc2_bias_grad: float32 [1152], P('fsdp')
Inputs may be any that keep to these rules, and one draw needn't show every extreme that they name: `segment_ids`: each row holds whole images one after another, numbered from 0 in order: eight images of 32 tokens, or two of 128 tokens, or one of 128 tokens among four of 32 tokens. Some row holds eight images and some row holds two. `tokens`: token features.
All inputs are finite; a program needn't handle non-finite values.
Results may differ from a plain program's by a relative error of at most 0.02.
The roundings to bfloat16 on the way count: a program that leaves them out, or rounds other values in their place, can miss the bound.
Values may be sent and summed in bfloat16 or wider, within the bound.
A program may use at most 384 MiB of HBM per device.

v0:
```python
import jax
import jax.numpy as jnp
from jax import lax
from jax.sharding import PartitionSpec as P

HEADS = 16
HEAD_DIM = 72


root_half = 0.7978845608028654
norm_eps = 1e-06
masked_score = -1e30


def gelu_tanh(stream):
    return (
        0.5 * stream * (1.0 + jnp.tanh(root_half * (stream + 0.044715 * stream * stream * stream)))
    )


def gelu_slope(stream):
    tanh_inner = jnp.tanh(root_half * (stream + 0.044715 * stream * stream * stream))
    return 0.5 * (1.0 + tanh_inner) + 0.5 * stream * (1.0 - tanh_inner * tanh_inner) * root_half * (
        1.0 + 3.0 * 0.044715 * stream * stream
    )


def normalize(stream):
    centre = jnp.mean(stream, axis=-1, keepdims=True)
    centred = stream - centre
    inv_std = lax.rsqrt(jnp.mean(centred * centred, axis=-1, keepdims=True) + norm_eps)
    return (centred * inv_std, inv_std)


def normalize_back(incoming, normed, inv_std):
    return inv_std * (
        incoming
        - jnp.mean(incoming, axis=-1, keepdims=True)
        - normed * jnp.mean(incoming * normed, axis=-1, keepdims=True)
    )


def head_scores(projected, same_doc, head_index, model_width):
    query_part = lax.dynamic_slice_in_dim(projected, head_index * HEAD_DIM, HEAD_DIM, 1)
    key_part = lax.dynamic_slice_in_dim(projected, model_width + head_index * HEAD_DIM, HEAD_DIM, 1)
    value_part = lax.dynamic_slice_in_dim(
        projected, 2 * model_width + head_index * HEAD_DIM, HEAD_DIM, 1
    )
    raw_scores = jnp.einsum(
        "qd,kd->qk", query_part, key_part, preferred_element_type=jnp.float32
    ) * HEAD_DIM ** (-0.5)
    return (jnp.where(same_doc, raw_scores, masked_score), query_part, key_part, value_part)


def merge_heads(stacked, model_width):
    return jnp.transpose(stacked, (1, 0, 2)).reshape(stacked.shape[1], model_width)


def attend_row(projected, segments_row, model_width):
    same_doc = segments_row[:, None] == segments_row[None, :]

    def one_head(head_index):
        scores, query_part, key_part, value_part = head_scores(
            projected, same_doc, head_index, model_width
        )
        top_score = jnp.max(scores, axis=-1, keepdims=True)
        exp_scores = jnp.exp(scores - top_score)
        denominator = jnp.sum(exp_scores, axis=-1, keepdims=True)
        probabilities = (exp_scores / denominator).astype(jnp.bfloat16)
        mixed_heads = jnp.dot(probabilities, value_part, preferred_element_type=jnp.float32)
        return (mixed_heads, (top_score + jnp.log(denominator))[:, 0])

    mixed_heads, log_total = lax.map(one_head, jnp.arange(HEADS))
    return (merge_heads(mixed_heads, model_width).astype(jnp.bfloat16), log_total)


def attend_back(projected, segments_row, log_total, d_mixed, model_width):
    same_doc = segments_row[:, None] == segments_row[None, :]
    head_scale = HEAD_DIM ** (-0.5)

    def one_head(head_index):
        scores, query_part, key_part, value_part = head_scores(
            projected, same_doc, head_index, model_width
        )
        d_head = lax.dynamic_slice_in_dim(d_mixed, head_index * HEAD_DIM, HEAD_DIM, 1)
        lse_row = lax.dynamic_index_in_dim(log_total, head_index, 0, keepdims=False)
        probabilities = jnp.exp(scores - lse_row[:, None])
        prob_low = probabilities.astype(jnp.bfloat16)
        d_probs = jnp.einsum("qd,kd->qk", d_head, value_part, preferred_element_type=jnp.float32)
        d_value = jnp.einsum("qk,qd->kd", prob_low, d_head, preferred_element_type=jnp.float32)
        d_scores = (
            probabilities * (d_probs - jnp.sum(d_probs * probabilities, axis=-1, keepdims=True))
        ).astype(jnp.bfloat16)
        d_query = (
            jnp.einsum("qk,kd->qd", d_scores, key_part, preferred_element_type=jnp.float32)
            * head_scale
        )
        d_key = (
            jnp.einsum("qk,qd->kd", d_scores, query_part, preferred_element_type=jnp.float32)
            * head_scale
        )
        return (d_query, d_key, d_value)

    d_query, d_key, d_value = lax.map(one_head, jnp.arange(HEADS))
    merged = [
        merge_heads(d_query, model_width),
        merge_heads(d_key, model_width),
        merge_heads(d_value, model_width),
    ]
    return jnp.concatenate(merged, axis=-1).astype(jnp.bfloat16)


def on_device(
    tokens,
    cond,
    segment_ids,
    ada_weight,
    ada_bias,
    qkv_weight,
    qv_bias,
    proj_weight,
    proj_bias,
    fc1_weight,
    fc1_bias,
    fc2_weight,
    fc2_bias,
    out_grad,
):
    row_count, seq_len, model_width = tokens.shape
    ff_width = fc1_weight.shape[1]
    stream = tokens.astype(jnp.float32)
    cond_float = cond.astype(jnp.float32)
    cond_act = (cond_float / (1.0 + jnp.exp(-cond_float))).astype(jnp.bfloat16)
    ada_full, ada_bias_full = (
        lax.all_gather(ada_weight, "fsdp", axis=0, tiled=True),
        lax.all_gather(ada_bias, "fsdp", axis=0, tiled=True),
    )
    modulation = jnp.dot(
        cond_act, ada_full, preferred_element_type=jnp.float32
    ) + ada_bias_full.astype(jnp.float32)
    pieces = [
        modulation[:, None, section * model_width : (section + 1) * model_width]
        for section in range(6)
    ]
    shift_one, scale_one, gate_one, shift_two, scale_two, gate_two = pieces
    qkv_full, qv_bias_full, proj_full, proj_bias_full = (
        lax.all_gather(qkv_weight, "fsdp", axis=0, tiled=True),
        lax.all_gather(qv_bias, "fsdp", axis=0, tiled=True),
        lax.all_gather(proj_weight, "fsdp", axis=0, tiled=True),
        lax.all_gather(proj_bias, "fsdp", axis=0, tiled=True),
    )
    normed_one, inv_one = normalize(stream)
    hidden_one = (normed_one * (1.0 + scale_one) + shift_one).astype(jnp.bfloat16)
    qv_float = qv_bias_full.astype(jnp.float32)
    qkv_bias = jnp.concatenate(
        [qv_float[:model_width], jnp.zeros((model_width,), jnp.float32), qv_float[model_width:]]
    )
    projected = (
        jnp.dot(hidden_one, qkv_full, preferred_element_type=jnp.float32) + qkv_bias
    ).astype(jnp.bfloat16)

    def row_forward(row_items):
        return attend_row(row_items[0], row_items[1], model_width)

    mixed_rows, log_total = lax.map(row_forward, (projected, segment_ids))
    branch_one = jnp.dot(
        mixed_rows, proj_full, preferred_element_type=jnp.float32
    ) + proj_bias_full.astype(jnp.float32)
    resid_one = stream + gate_one * branch_one
    fc1_full, fc1_bias_full, fc2_full, fc2_bias_full = (
        lax.all_gather(fc1_weight, "fsdp", axis=0, tiled=True),
        lax.all_gather(fc1_bias, "fsdp", axis=0, tiled=True),
        lax.all_gather(fc2_weight, "fsdp", axis=0, tiled=True),
        lax.all_gather(fc2_bias, "fsdp", axis=0, tiled=True),
    )
    normed_two, inv_two = normalize(resid_one)
    hidden_two = (normed_two * (1.0 + scale_two) + shift_two).astype(jnp.bfloat16)
    pre_act = jnp.dot(
        hidden_two, fc1_full, preferred_element_type=jnp.float32
    ) + fc1_bias_full.astype(jnp.float32)
    active = gelu_tanh(pre_act).astype(jnp.bfloat16)
    branch_two = jnp.dot(
        active, fc2_full, preferred_element_type=jnp.float32
    ) + fc2_bias_full.astype(jnp.float32)
    output = (resid_one + gate_two * branch_two).astype(jnp.bfloat16)
    d_out = out_grad.astype(jnp.float32)
    fc1_back, fc2_back = (
        lax.all_gather(fc1_weight, "fsdp", axis=0, tiled=True),
        lax.all_gather(fc2_weight, "fsdp", axis=0, tiled=True),
    )
    d_gate_two = jnp.sum(d_out * branch_two, axis=1)
    d_branch_two = (d_out * gate_two).astype(jnp.bfloat16)
    fc2_shard = lax.psum_scatter(
        jnp.einsum("rsf,rsd->fd", active, d_branch_two, preferred_element_type=jnp.float32).astype(
            jnp.bfloat16
        ),
        "fsdp",
        scatter_dimension=0,
        tiled=True,
    )
    grad_fc2_bias = jnp.sum(d_branch_two.astype(jnp.float32), axis=(0, 1))
    d_active = jnp.einsum("rsd,fd->rsf", d_branch_two, fc2_back, preferred_element_type=jnp.float32)
    d_pre = (d_active * gelu_slope(pre_act)).astype(jnp.bfloat16)
    grad_fc1_bias = jnp.sum(d_pre.astype(jnp.float32), axis=(0, 1))
    d_hidden_two = jnp.einsum("rsf,ef->rse", d_pre, fc1_back, preferred_element_type=jnp.float32)
    d_scale_two = jnp.sum(d_hidden_two * normed_two, axis=1)
    d_shift_two = jnp.sum(d_hidden_two, axis=1)
    d_resid = d_out + normalize_back(d_hidden_two * (1.0 + scale_two), normed_two, inv_two)
    qkv_back, proj_back = (
        lax.all_gather(qkv_weight, "fsdp", axis=0, tiled=True),
        lax.all_gather(proj_weight, "fsdp", axis=0, tiled=True),
    )
    d_gate_one = jnp.sum(d_resid * branch_one, axis=1)
    d_branch_one = (d_resid * gate_one).astype(jnp.bfloat16)
    grad_proj_bias = jnp.sum(d_branch_one.astype(jnp.float32), axis=(0, 1))
    d_mixed = jnp.einsum(
        "rsd,ed->rse", d_branch_one, proj_back, preferred_element_type=jnp.float32
    ).astype(jnp.bfloat16)

    def row_backward(row_items):
        return attend_back(row_items[0], row_items[1], row_items[2], row_items[3], model_width)

    d_projected = lax.map(row_backward, (projected, segment_ids, log_total, d_mixed))
    d_proj_float = d_projected.astype(jnp.float32)
    grad_qv_bias = jnp.concatenate(
        [
            jnp.sum(d_proj_float[..., :model_width], axis=(0, 1)),
            jnp.sum(d_proj_float[..., 2 * model_width :], axis=(0, 1)),
        ]
    )
    d_hidden_one = jnp.einsum(
        "rsf,ef->rse", d_projected, qkv_back, preferred_element_type=jnp.float32
    )
    d_scale_one = jnp.sum(d_hidden_one * normed_one, axis=1)
    d_shift_one = jnp.sum(d_hidden_one, axis=1)
    tokens_grad = (
        d_resid + normalize_back(d_hidden_one * (1.0 + scale_one), normed_one, inv_one)
    ).astype(jnp.bfloat16)
    d_modulation = jnp.concatenate(
        [d_shift_one, d_scale_one, d_gate_one, d_shift_two, d_scale_two, d_gate_two], axis=-1
    ).astype(jnp.bfloat16)
    grad_ada_bias = jnp.sum(d_modulation.astype(jnp.float32), axis=0)
    terms = [
        jnp.einsum("rse,rsf->ef", hidden_one, d_projected, preferred_element_type=jnp.float32),
        jnp.einsum("rse,rsd->ed", mixed_rows, d_branch_one, preferred_element_type=jnp.float32),
        jnp.einsum("rse,rsf->ef", hidden_two, d_pre, preferred_element_type=jnp.float32),
    ]
    terms.append(
        jnp.einsum("rd,re->de", cond_act, d_modulation, preferred_element_type=jnp.float32)
    )
    wide_shard = lax.psum_scatter(
        jnp.concatenate(terms, axis=1).astype(jnp.bfloat16), "fsdp", scatter_dimension=0, tiled=True
    ).astype(jnp.float32)
    qkv_shard = wide_shard[:, : 3 * model_width]
    proj_shard = wide_shard[:, 3 * model_width : 4 * model_width]
    fc1_shard = wide_shard[:, 4 * model_width : 4 * model_width + ff_width]
    ada_shard = wide_shard[:, 4 * model_width + ff_width :]
    bias_shards = (
        lax.psum_scatter(
            grad_ada_bias.astype(jnp.bfloat16), "fsdp", scatter_dimension=0, tiled=True
        ).astype(jnp.float32),
        lax.psum_scatter(
            grad_qv_bias.astype(jnp.bfloat16), "fsdp", scatter_dimension=0, tiled=True
        ).astype(jnp.float32),
        lax.psum_scatter(
            grad_proj_bias.astype(jnp.bfloat16), "fsdp", scatter_dimension=0, tiled=True
        ).astype(jnp.float32),
        lax.psum_scatter(
            grad_fc1_bias.astype(jnp.bfloat16), "fsdp", scatter_dimension=0, tiled=True
        ).astype(jnp.float32),
        lax.psum_scatter(
            grad_fc2_bias.astype(jnp.bfloat16), "fsdp", scatter_dimension=0, tiled=True
        ).astype(jnp.float32),
    )
    summed = (
        lax.psum(ada_shard.astype(jnp.bfloat16), "dp").astype(jnp.float32),
        lax.psum(bias_shards[0].astype(jnp.bfloat16), "dp").astype(jnp.float32),
        lax.psum(qkv_shard.astype(jnp.bfloat16), "dp").astype(jnp.float32),
        lax.psum(bias_shards[1].astype(jnp.bfloat16), "dp").astype(jnp.float32),
        lax.psum(proj_shard.astype(jnp.bfloat16), "dp").astype(jnp.float32),
        lax.psum(bias_shards[2].astype(jnp.bfloat16), "dp").astype(jnp.float32),
        lax.psum(fc1_shard.astype(jnp.bfloat16), "dp").astype(jnp.float32),
        lax.psum(bias_shards[3].astype(jnp.bfloat16), "dp").astype(jnp.float32),
        lax.psum(fc2_shard, "dp").astype(jnp.float32),
        lax.psum(bias_shards[4].astype(jnp.bfloat16), "dp").astype(jnp.float32),
    )
    return (
        output,
        tokens_grad,
        summed[0],
        summed[1],
        summed[2],
        summed[3],
        summed[4],
        summed[5],
        summed[6],
        summed[7],
        summed[8],
        summed[9],
    )


def solution(mesh):
    in_specs = (
        P(("fsdp", "dp"), None, None),
        P(("fsdp", "dp"), None),
        P(("fsdp", "dp"), None),
        P("fsdp", None),
        P("fsdp"),
        P("fsdp", None),
        P("fsdp"),
        P("fsdp", None),
        P("fsdp"),
        P("fsdp", None),
        P("fsdp"),
        P("fsdp", None),
        P("fsdp"),
        P(("fsdp", "dp"), None, None),
    )
    out_specs = (
        P(("fsdp", "dp"), None, None),
        P(("fsdp", "dp"), None, None),
        P("fsdp", None),
        P("fsdp"),
        P("fsdp", None),
        P("fsdp"),
        P("fsdp", None),
        P("fsdp"),
        P("fsdp", None),
        P("fsdp"),
        P("fsdp", None),
        P("fsdp"),
    )
    return jax.shard_map(
        on_device, mesh=mesh, in_specs=in_specs, out_specs=out_specs, check_vma=False
    )
```

profile of v0, /device:TPU:0, one launch (start us, length us, event | category | flops | bytes accessed | tf_op | source)
XLA Modules:
  0.0 1530.7 jit_solution(7931803233597457962)
XLA Ops:
  15.8 67.0 %all-reduce.12 = (bf16[2304]{0:T(1024)(128)(2,1)S(1)}, bf16[6912]{0:T(1024)(128)(2,1)S(1)}, bf16[1152]{0:T(1024)(128)(2,1)S(1)}, bf16[1152]{0:T(1024)(128)(2,1)S(1)}, bf16[4608]{0:T(1024)(128)(2,1)S(1)}) all-reduce(bf16[2304]{0:T(1024)(128)(2,1)S(1)} %dynamic-update-slice.1, ...), channel_id=1, replica_groups=mesh['fsdp'=16,'dp'=2] {'fsdp'}, use_global_device_ids=true, to_apply=%add.1 | all-reduce | flops 16128 | bytes 64512
  85.1 49.5 %all-gather.6.cloned.1.call-done = bf16[1152,6912]{1,0:T(8,128)(2,1)} async-done(((bf16[72,6912]{1,0:T(8,128)(2,1)}), bf16[1152,6912]{1,0:T(8,128)(2,1)}) %all-gather.6.cloned.1.call-update) | async-done | bytes 15925264 | tf_op jit(solution)/shard_map/all_gather | solution.py:135
  134.6 7.7 convolution_reduce_fusion
  143.1 63.6 %all-gather.8.cloned.1.call-done = bf16[1152,3456]{1,0:T(8,128)(2,1)} async-done(((bf16[72,3456]{1,0:T(8,128)(2,1)}), bf16[1152,3456]{1,0:T(8,128)(2,1)}) %all-gather.8.cloned.1.call-update) | async-done | bytes 7962640 | tf_op jit(solution)/shard_map/all_gather | solution.py:147
  206.7 7.2 fusion.37
  214.0 82.1 %while.50 = (s32[]{:T(128)}, bf16[16,256,72]{1,2,0:T(8,128)(2,1)S(1)}, f32[16,256]{1,0:T(8,128)}, s32[16]{0:T(128)S(1)}, bf16[256,3456]{1,0:T(8,128)(2,1)}, /*in...) while((s32[]{:T(128)}, ...), condition=%wide.region_5.6_spmd.clone, body=%wide.region_2.5_spmd.clone.sunk | while | flops 19463948 | bytes 1069367 | solution.py:73
  296.1 3.0 fusion.88
  300.4 39.4 %all-gather.12.cloned.1.call-done = bf16[1152,4608]{1,0:T(8,128)(2,1)} async-done(((bf16[72,4608]{1,0:T(8,128)(2,1)}), bf16[1152,4608]{1,0:T(8,128)(2,1)}) %all-gather.12.cloned.1.call-update) | async-done | bytes 10616848 | tf_op jit(solution)/shard_map/all_gather | solution.py:171
  339.8 9.1 convolution_add_fusion
  349.0 80.0 %all-gather.14.cloned.1.call-done = bf16[4608,1152]{1,0:T(8,128)(2,1)} async-done(((bf16[288,1152]{1,0:T(8,128)(2,1)}), bf16[4608,1152]{1,0:T(8,128)(2,1)}) %all-gather.14.cloned.1.call-update) | async-done | bytes 10616848 | tf_op jit(solution)/shard_map/all_gather | solution.py:173
  428.9 8.8 fusion.92
  437.7 6.6 convolution_convert_fusion.1
  444.3 3.9 fusion.85
  448.2 10.6 fusion.59
  458.8 2.4 fusion.87
  461.2 2.4 convolution_convert_fusion.3
  465.7 161.9 %while.51 = (s32[]{:T(128)}, bf16[16,256,72]{1,2,0:T(8,128)(2,1)S(1)}, bf16[16,256,72]{1,2,0:T(8,128)(2,1)S(1)}, bf16[16,256,72]{1,2,0:T(8,128)(2,1)S(1)}, s32[1...) while((s32[]{:T(128)}, ...), condition=%wide.region_12.13_spmd.clone, body=%wide.region_10.12_spmd.clone.sunk | while | flops 47877904 | bytes 2654166 | solution.py:104
  628.5 6.4 convolution_convert_fusion.2
  635.0 7.0 fusion.56
  645.2 2.7 fusion.61
  649.4 4.1 copy.27
  653.6 5.9 multiply_convert_fusion.1
  659.5 24.5 %pad_maximum_fusion = bf16[1152,16128]{1,0:T(8,128)(2,1)} fusion(bf16[1152,6912]{1,0:T(8,128)(2,1)} %multiply_convert_fusion.1, bf16[1152,4608]{1,0:T(8,128)(2,1)} %convolution_convert_fusion.1, bf16[1152,1152]{1,0:T(8,128)(2,1)S(1)} %copy.27, bf16[1152,3456]{1,0:T(8,128)(2,1)} %convolution_convert_fusion.2), kind=kLoop, calls=%fused_computation.46 | loop fusion | flops 148635648 | bytes 74317824 | tf_op jit(solution)/shard_map/concatenate | solution.py:252
  685.1 10.6 convolution_convert_fusion
  696.4 608.9 %all-reduce.18.cloned.1.call-done = bf16[1152,16128]{1,0:T(8,128)(2,1)} async-done(((bf16[1152,16128]{1,0:T(8,128)(2,1)}), bf16[1152,16128]{1,0:T(8,128)(2,1)}) %all-reduce.18.cloned.1.call-update) | async-done | bytes 37158928
  1307.1 2.2 dynamic-slice.21
  1309.3 2.6 dynamic-slice.18
  1313.9 115.9 %reduce-scatter.2.cloned.1.call-done = bf16[288,1152]{1,0:T(8,128)(2,1)} async-done(((bf16[4608,1152]{1,0:T(8,128)(2,1)}), bf16[288,1152]{1,0:T(8,128)(2,1)}) %reduce-scatter.2.cloned.1.call-update) | async-done | bytes 663568 | tf_op jit(solution)/shard_map/reduce_scatter | solution.py:193
  1432.2 60.2 %all-reduce.11 = (bf16[6912]{0:T(1024)(128)(2,1)S(1)}, bf16[2304]{0:T(1024)(128)(2,1)S(1)}, bf16[1152]{0:T(1024)(128)(2,1)S(1)}, bf16[4608]{0:T(1024)(128)(2,1)S(1)}, bf16[1152]{0:T(1024)(128)(2,1)S(1)}) all-reduce(bf16[6912]{0:T(1024)(128)(2,1)S(1)} %copy-done.17, ...), channel_id=3, replica_groups=mesh['fsdp'=16,'dp'=2] {'fsdp'}, use_global_device_ids=true, to_apply=%region_23.24.clone | all-reduce | flops 16128 | bytes 64512
  1492.8 5.1 all-reduce.13
  1500.6 15.1 all-reduce.20.cloned.1.call-done
  1517.4 2.7 convert_element_type.206
  (462 shorter events, 221.0 us)
Async XLA Ops:
  7.2 6.7 copy-start.23
  7.2 7.4 copy-start.42
  7.2 7.6 copy-start.43
  7.2 7.8 copy-start.44
  7.2 8.1 copy-start.38
  7.2 8.3 copy-start.39
  7.3 77.4 %copy-start = (bf16[1,256,1152]{2,1,0:T(8,128)(2,1)S(1)}, bf16[1,256,1152]{2,1,0:T(8,128)(2,1)}, u32[]{:S(2)}) copy-start(bf16[1,256,1152]{2,1,0:T(8,128)(2,1)} %param.18) | copy-start | bytes 1769476
  7.3 127.4 %all-gather.6.cloned.1.call-start = ((), (), s32[]{:S(2)}) async-start(), calls=%async_computation.1 | async-start | bytes 16920576 | tf_op jit(solution)/shard_map/all_gather | solution.py:135
  8.0 198.7 %all-gather.8.cloned.1.call-start = ((), (), s32[]{:S(2)}) async-start(), calls=%async_computation.2 | async-start | bytes 8460288 | tf_op jit(solution)/shard_map/all_gather | solution.py:147
  8.7 287.3 %all-gather.10.cloned.1.call-start = ((), (), s32[]{:S(2)}) async-start(), calls=%async_computation.3 | async-start | bytes 2820096 | tf_op jit(solution)/shard_map/all_gather | solution.py:149
  9.5 330.4 %all-gather.12.cloned.1.call-start = ((), (), s32[]{:S(2)}) async-start(), calls=%async_computation.4 | async-start | bytes 11280384 | tf_op jit(solution)/shard_map/all_gather | solution.py:171
  10.1 418.9 %all-gather.14.cloned.1.call-start = ((), (), s32[]{:S(2)}) async-start(), calls=%async_computation.5 | async-start | bytes 11280384 | tf_op jit(solution)/shard_map/all_gather | solution.py:173
  10.6 1294.7 %all-reduce.18.cloned.1.call-start = ((), (), s32[]{:S(2)}) async-start(), calls=%async_computation.7 | async-start | bytes 74317824
  84.8 121.9 %copy-start.28 = (f32[256]{0:T(256)}, f32[256]{0:T(256)S(1)}, u32[]{:S(2)}) copy-start(f32[256]{0:T(256)S(1)} %broadcast_multiply_fusion.5) | copy-start | bytes 3076
  85.1 121.6 %copy-start.32 = (f32[256]{0:T(256)}, f32[256]{0:T(256)S(1)}, u32[]{:S(2)}) copy-start(f32[256]{0:T(256)S(1)} %add_rsqrt_fusion.1) | copy-start | bytes 3076
  143.1 70.9 %copy-start.30 = (f32[1152]{0:T(1024)}, f32[1152]{0:T(1024)S(1)}, u32[]{:S(2)}) copy-start(f32[1152]{0:T(1024)S(1)} %get-tuple-element.294) | copy-start | bytes 13828
  206.7 7.3 copy-start.41
  428.9 8.8 copy-start.14
  428.9 8.8 copy-start.22
  428.9 8.8 copy-start.26
  437.7 6.6 copy-start.40
  448.2 10.6 copy-start.13
  465.6 162.9 %copy-start.29 = (f32[256]{0:T(256)S(1)}, f32[256]{0:T(256)}, u32[]{:S(2)}) copy-start(f32[256]{0:T(256)} %copy-done.28) | copy-start | bytes 3076
  521.4 4.9 copy-start.46
  561.9 4.9 copy-start.46
  627.5 7.4 copy-start.2
  628.5 6.5 copy-start.33
  684.0 745.7 %reduce-scatter.2.cloned.1.call-start = ((), (), s32[]{:S(2)}) async-start(), calls=%async_computation.6 | async-start | bytes 11280384 | tf_op jit(solution)/shard_map/reduce_scatter | solution.py:193
  695.7 820.0 %all-reduce.20.cloned.1.call-start = ((), (), s32[]{:S(2)}) async-start(), calls=%async_computation.8 | async-start | bytes 5971968 | tf_op jit(solution)/shard_map/psum | solution.py:276
  1311.9 119.8 %copy-start.3 = (bf16[16,256,72]{1,2,0:T(8,128)(2,1)S(1)}, bf16[16,256,72]{1,2,0:T(8,128)(2,1)}, u32[]{:S(2)}) copy-start(bf16[16,256,72]{1,2,0:T(8,128)(2,1)} %copy-done.2) | copy-start | bytes 1769476
  1311.9 119.8 %copy-start.5 = (bf16[16,256,72]{1,2,0:T(8,128)(2,1)S(1)}, bf16[16,256,72]{1,2,0:T(8,128)(2,1)}, u32[]{:S(2)}) copy-start(bf16[16,256,72]{1,2,0:T(8,128)(2,1)} %copy-done.4) | copy-start | bytes 1769476
  1311.9 119.9 %copy-start.7 = (bf16[16,256,72]{1,2,0:T(8,128)(2,1)S(1)}, bf16[16,256,72]{1,2,0:T(8,128)(2,1)}, u32[]{:S(2)}) copy-start(bf16[16,256,72]{1,2,0:T(8,128)(2,1)} %copy-done.6) | copy-start | bytes 1769476
  (53 other events, 178.8 us)
Sparse Core Ops, SparseCore 0:
  10.3 124.3 all-gather.5
  136.8 69.8 all-gather.7
  208.9 41.8 all-gather.9
  252.9 86.8 all-gather.11
  342.0 86.8 all-gather.13
  684.2 621.1 all-reduce.17
  1309.4 120.2 reduce-scatter.1
  1433.5 82.1 all-reduce.19
where the time goes:
time: 1540 us; the launch traced here: 1530 us
  waiting for transfers between devices  976 us (63%)
  matrix products  221 us (14%)
  blocking collectives  132 us (9%)
  local copies, waits for them, and re-layouts  73.3 us (5%)
  loops' own time  54.4 us (4%)
  other arithmetic  53 us (3%)
  between operations  20.2 us (1%)
    unnamed x9, waiting for transfers between devices  612 us
    unnamed x2, blocking collectives  127 us
    reduce_scatter x1, waiting for transfers between devices, on_device(): lax.psum_scatter(jnp.einsum('rsf,rsd->fd', active, d_branch_two, preferre...  116 us
    all_gather x1, waiting for transfers between devices, on_device(): lax.all_gather(fc2_weight, 'fsdp', axis=0, tiled=True)  80 us
    all_gather x1, waiting for transfers between devices, on_device(): lax.all_gather(qkv_weight, 'fsdp', axis=0, tiled=True)  63.6 us
    all_gather x1, waiting for transfers between devices, on_device(): lax.all_gather(ada_weight, 'fsdp', axis=0, tiled=True)  49.5 us
    another operation x1, loops' own time, attend_back(): d_query, d_key, d_value = lax.map(one_head, jnp.arange(HEADS))  43.4 us
    dot_general x32, matrix products, head_scores(): jnp.einsum('qd,kd->qk', query_part, key_part, preferred_element_type=jnp....  40.5 us
  transfers between devices with their start and end apart: 8, of which 7 were waited for; matrix products, arithmetic and copies ran while one was open for 8% of the time, Pallas kernels for 0%

commit v1 on v0

--- a/solution.py
+++ b/solution.py
@@ -131,13 +131,23 @@
     stream = tokens.astype(jnp.float32)
     cond_float = cond.astype(jnp.float32)
     cond_act = (cond_float / (1.0 + jnp.exp(-cond_float))).astype(jnp.bfloat16)
-    ada_full, ada_bias_full = (
-        lax.all_gather(ada_weight, "fsdp", axis=0, tiled=True),
-        lax.all_gather(ada_bias, "fsdp", axis=0, tiled=True),
-    )
-    modulation = jnp.dot(
-        cond_act, ada_full, preferred_element_type=jnp.float32
-    ) + ada_bias_full.astype(jnp.float32)
+    fsdp_at, dp_at = lax.axis_index("fsdp"), lax.axis_index("dp")
+    dp_size = lax.axis_size("dp")
+    slice_width, bias_width = ada_weight.shape[0], ada_bias.shape[0]
+    act_all = lax.all_gather(cond_act, ("fsdp", "dp"), axis=0, tiled=True)
+    act_mine = lax.dynamic_slice_in_dim(act_all, fsdp_at * slice_width, slice_width, 1)
+    partial = jnp.dot(act_mine, ada_weight, preferred_element_type=jnp.float32)
+    bias_row = lax.dynamic_update_slice_in_dim(
+        jnp.zeros((6 * model_width,), jnp.float32),
+        ada_bias.astype(jnp.float32),
+        fsdp_at * bias_width,
+        0,
+    )
+    partial = (partial + bias_row).reshape(-1, dp_size, row_count, 6 * model_width)
+    partial = lax.dynamic_index_in_dim(partial, dp_at, 1, keepdims=False)
+    modulation = lax.psum_scatter(
+        partial.reshape(-1, 6 * model_width), "fsdp", scatter_dimension=0, tiled=True
+    )
     pieces = [
         modulation[:, None, section * model_width : (section + 1) * model_width]
         for section in range(6)
@@ -239,26 +249,29 @@
     d_modulation = jnp.concatenate(
         [d_shift_one, d_scale_one, d_gate_one, d_shift_two, d_scale_two, d_gate_two], axis=-1
     ).astype(jnp.bfloat16)
-    grad_ada_bias = jnp.sum(d_modulation.astype(jnp.float32), axis=0)
-    terms = [
-        jnp.einsum("rse,rsf->ef", hidden_one, d_projected, preferred_element_type=jnp.float32),
-        jnp.einsum("rse,rsd->ed", mixed_rows, d_branch_one, preferred_element_type=jnp.float32),
-        jnp.einsum("rse,rsf->ef", hidden_two, d_pre, preferred_element_type=jnp.float32),
-    ]
-    terms.append(
-        jnp.einsum("rd,re->de", cond_act, d_modulation, preferred_element_type=jnp.float32)
-    )
-    wide_shard = lax.psum_scatter(
-        jnp.concatenate(terms, axis=1).astype(jnp.bfloat16), "fsdp", scatter_dimension=0, tiled=True
-    ).astype(jnp.float32)
-    qkv_shard = wide_shard[:, : 3 * model_width]
-    proj_shard = wide_shard[:, 3 * model_width : 4 * model_width]
-    fc1_shard = wide_shard[:, 4 * model_width : 4 * model_width + ff_width]
-    ada_shard = wide_shard[:, 4 * model_width + ff_width :]
+    d_mod_all = lax.all_gather(d_modulation, ("fsdp", "dp"), axis=0, tiled=True)
+    grad_ada = jnp.einsum("rd,re->de", act_mine, d_mod_all, preferred_element_type=jnp.float32)
+    grad_ada_bias = jnp.sum(
+        lax.dynamic_slice_in_dim(d_mod_all, fsdp_at * bias_width, bias_width, 1).astype(jnp.float32),
+        axis=0,
+    )
+
+    def owners(term):
+        return lax.psum_scatter(
+            term.astype(jnp.bfloat16), "fsdp", scatter_dimension=0, tiled=True
+        )
+
+    qkv_shard = owners(
+        jnp.einsum("rse,rsf->ef", hidden_one, d_projected, preferred_element_type=jnp.float32)
+    )
+    proj_shard = owners(
+        jnp.einsum("rse,rsd->ed", mixed_rows, d_branch_one, preferred_element_type=jnp.float32)
+    )
+    fc1_shard = owners(
+        jnp.einsum("rse,rsf->ef", hidden_two, d_pre, preferred_element_type=jnp.float32)
+    )
     bias_shards = (
-        lax.psum_scatter(
-            grad_ada_bias.astype(jnp.bfloat16), "fsdp", scatter_dimension=0, tiled=True
-        ).astype(jnp.float32),
+        None,
         lax.psum_scatter(
             grad_qv_bias.astype(jnp.bfloat16), "fsdp", scatter_dimension=0, tiled=True
         ).astype(jnp.float32),
@@ -273,8 +286,8 @@
         ).astype(jnp.float32),
     )
     summed = (
-        lax.psum(ada_shard.astype(jnp.bfloat16), "dp").astype(jnp.float32),
-        lax.psum(bias_shards[0].astype(jnp.bfloat16), "dp").astype(jnp.float32),
+        grad_ada,
+        grad_ada_bias,
         lax.psum(qkv_shard.astype(jnp.bfloat16), "dp").astype(jnp.float32),
         lax.psum(bias_shards[1].astype(jnp.bfloat16), "dp").astype(jnp.float32),
         lax.psum(proj_shard.astype(jnp.bfloat16), "dp").astype(jnp.float32),

time: 1540 us -> 1130 us (0.73)
  waiting for transfers between devices: 976 us -> 502 us
  blocking collectives: 132 us -> 268 us
  local copies, waits for them, and re-layouts: 73.3 us -> 29 us
  other arithmetic: 53 us -> 19.3 us
    unnamed x9 -> x13, waiting for transfers between devices: 612 us -> 24.7 us
    all_gather x0 -> x2, blocking collectives: none -> 143 us  [the longest x1 73 us: on_device(): d_mod_all = lax.all_gather(d_modulation, ('fsdp', 'dp'), axis=0, tiled=True)]
    reduce_scatter x0 -> x1, waiting for transfers between devices: none -> 109 us  [owners(): lax.psum_scatter(term.astype(jnp.bfloat16), 'fsdp', scatter_dimension=0,...]
    all_gather x1 -> x0, waiting for transfers between devices: 49.5 us -> none  [on_device(): lax.all_gather(ada_weight, 'fsdp', axis=0, tiled=True)]
    all_gather x1, waiting for transfers between devices: 39.4 us -> 85.2 us  [on_device(): lax.all_gather(fc1_weight, 'fsdp', axis=0, tiled=True)]
    concatenate x1 -> x0, other arithmetic: 24.5 us -> none  [on_device(): jnp.concatenate(terms, axis=1).astype(jnp.bfloat16)]
    dynamic_update_slice x16, local copies, waits for them, and re-layouts: 21.1 us -> 0.69 us  [attend_row(): mixed_heads, log_total = lax.map(one_head, jnp.arange(HEADS))]
  transfers between devices with their start and end apart: 8 -> 10, of which waited for: 7 -> 7; matrix products, arithmetic and copies ran while one was open for 8% -> 22% of each run, Pallas kernels for 0% -> 0%
where the time goes in v1:
time: 1130 us; the launch traced here: 1120 us
  waiting for transfers between devices  502 us (44%)
  blocking collectives  268 us (24%)
  matrix products  225 us (20%)
  loops' own time  53.6 us (5%)
  local copies, waits for them, and re-layouts  29 us (3%)
  other arithmetic  19.3 us (2%)
  between operations  18.9 us (2%)
    reduce_scatter x1, waiting for transfers between devices, on_device(): lax.psum_scatter(jnp.einsum('rsf,rsd->fd', active, d_branch_two, preferre...  124 us
    unnamed x2, blocking collectives  120 us
    reduce_scatter x1, waiting for transfers between devices, owners(): lax.psum_scatter(term.astype(jnp.bfloat16), 'fsdp', scatter_dimension=0,...  109 us
    all_gather x1, waiting for transfers between devices, on_device(): lax.all_gather(fc1_weight, 'fsdp', axis=0, tiled=True)  85.2 us
    all_gather x1, waiting for transfers between devices, on_device(): lax.all_gather(fc2_weight, 'fsdp', axis=0, tiled=True)  79.7 us
    all_gather x1, blocking collectives, on_device(): d_mod_all = lax.all_gather(d_modulation, ('fsdp', 'dp'), axis=0, tiled=True)  73 us
    all_gather x1, waiting for transfers between devices, on_device(): lax.all_gather(qkv_weight, 'fsdp', axis=0, tiled=True)  72.5 us
    all_gather x1, blocking collectives, on_device(): act_all = lax.all_gather(cond_act, ('fsdp', 'dp'), axis=0, tiled=True)  70.5 us
  transfers between devices with their start and end apart: 10, of which 7 were waited for; matrix products, arithmetic and copies ran while one was open for 22% of the time, Pallas kernels for 0%

profile of v1, /device:TPU:0, one launch (start us, length us, event | category | flops | bytes accessed | tf_op | source)
XLA Modules:
  0.0 1116.8 jit_solution(17571524379434750017)
XLA Ops:
  8.0 70.5 %all-gather = bf16[32,1,1152]{2,1,0:T(2,128)(2,1)S(1)} all-gather(bf16[1,1,1152]{2,1,0:T(2,128)(2,1)S(1)} %convert_bitcast_fusion), channel_id=1, replica_groups=mesh['fsdp'=16,'dp'=2] {'fsdp','dp'}, dimensions={0}, use_global_device_ids=true | all-gather | bytes 76032 | tf_op jit(solution)/shard_map/all_gather | solution.py:137
  87.5 57.8 %all-reduce.12 = (bf16[2304]{0:T(1024)(128)(2,1)S(1)}, bf16[1152]{0:T(1024)(128)(2,1)S(1)}, bf16[4608]{0:T(1024)(128)(2,1)S(1)}) all-reduce(bf16[2304]{0:T(1024)(128)(2,1)S(1)} %dynamic-update-slice, bf16[1152]{0:T(1024)(128)(2,1)S(1)} %dynamic-update-slice.1, ...), channel_id=1, replica_groups=mesh['fsdp'=16,'dp'=2] {'fsdp'}, use_global_device_ids=true, to_apply=%add | all-reduce | flops 8064 | bytes 32256
  145.8 22.1 %all-reduce.18.cloned.1.call-done = f32[16,6912]{1,0:T(8,128)} async-done(((f32[16,6912]{1,0:T(8,128)}), f32[16,6912]{1,0:T(8,128)}) %all-reduce.18.cloned.1.call-update) | async-done | bytes 442384
  169.6 72.5 %all-gather.7.cloned.1.call-done = bf16[1152,3456]{1,0:T(8,128)(2,1)} async-done(((bf16[72,3456]{1,0:T(8,128)(2,1)}), bf16[1152,3456]{1,0:T(8,128)(2,1)}) %all-gather.7.cloned.1.call-update) | async-done | bytes 7962640 | tf_op jit(solution)/shard_map/all_gather | solution.py:157
  242.1 6.0 fusion.37
  248.2 32.0 %while.50 = (s32[]{:T(128)}, bf16[16,256,72]{1,2,0:T(8,128)(2,1)S(1)}, f32[16,256]{1,0:T(8,128)S(1)}, s32[16]{0:T(128)S(1)}, bf16[256,3456]{1,0:T(8,128)(2,1)S(1...) while((s32[]{:T(128)}, ...), condition=%wide.region_6.7_spmd.clone, body=%wide.region_3.6_spmd.clone.sunk | while | flops 19463948 | bytes 1069367 | solution.py:73
  280.3 6.1 all-gather.9.cloned.1.call-done
  286.4 3.9 fusion.89
  290.5 85.2 %all-gather.11.cloned.1.call-done = bf16[1152,4608]{1,0:T(8,128)(2,1)} async-done(((bf16[72,4608]{1,0:T(8,128)(2,1)}), bf16[1152,4608]{1,0:T(8,128)(2,1)}) %all-gather.11.cloned.1.call-update) | async-done | bytes 10616848 | tf_op jit(solution)/shard_map/all_gather | solution.py:181
  375.7 9.1 convolution_add_fusion.1
  384.8 79.7 %all-gather.13.cloned.1.call-done = bf16[4608,1152]{1,0:T(8,128)(2,1)} async-done(((bf16[288,1152]{1,0:T(8,128)(2,1)}), bf16[4608,1152]{1,0:T(8,128)(2,1)}) %all-gather.13.cloned.1.call-update) | async-done | bytes 10616848 | tf_op jit(solution)/shard_map/all_gather | solution.py:183
  464.5 8.2 fusion.93
  472.7 8.3 fusion.60
  483.9 2.5 convolution_convert_fusion.3
  486.5 3.8 convolution_convert_fusion.4
  492.8 179.2 %while.51 = (s32[]{:T(128)}, bf16[16,256,72]{1,2,0:T(8,128)(2,1)}, bf16[16,256,72]{1,2,0:T(8,128)(2,1)}, bf16[16,256,72]{1,2,0:T(8,128)(2,1)}, s32[16]{0:T(128)S...) while((s32[]{:T(128)}, bf16[16,256,72]{1,2,0:T(8,128)(2,1)}, ...), condition=%wide.region_13.14_spmd.clone, body=%wide.region_11.13_spmd.clone.sunk | while | flops 47877904 | bytes 2653598 | solution.py:104
  498.7 1.8 fusion.138
  509.9 1.8 fusion.138
  521.1 1.8 fusion.138
  532.4 1.8 fusion.138
  543.6 1.8 fusion.138
  672.1 7.2 convolution_convert_fusion.2
  679.3 9.7 convolution_convert_fusion.1
  689.3 11.4 %convolution_convert_fusion = bf16[4608,1152]{1,0:T(8,128)(2,1)} fusion(bf16[1,256,1152]{2,1,0:T(8,128)(2,1)} %param.31, f32[1152]{0:T(1024)S(1)} %get-tuple-element.291, f32[256,4608]{1,0:T(8,128)} %convolution_add_fusion.1), kind=kOutput, calls=%fused_computation.46 | convolution fusion | flops 2734718976 | bytes 15929856 | tf_op jit(solution)/shard_map/rsf,rsd->fd/dot_general | solution.py:204
  705.9 62.1 %all-reduce.11 = (bf16[1152]{0:T(1024)(128)(2,1)S(1)}, bf16[2304]{0:T(1024)(128)(2,1)S(1)}, bf16[1152]{0:T(1024)(128)(2,1)S(1)}, bf16[4608]{0:T(1024)(128)(2,1)S(1)}, bf16[1152]{0:T(1024)(128)(2,1)S(1)}) all-reduce(bf16[1152]{0:T(1024)(128)(2,1)S(1)} %dynamic-update-slice.3, ...), channel_id=1, replica_groups=mesh['fsdp'=16,'dp'=2] {'fsdp'}, use_global_device_ids=true, to_apply=%add.3 | all-reduce | flops 10368 | bytes 41472
  768.3 5.2 all-reduce.13
  775.6 6.8 fusion.56
  783.7 10.3 fusion.59
  794.0 109.1 %reduce-scatter.9.cloned.1.call-done = bf16[72,4608]{1,0:T(8,128)(2,1)} async-done(((bf16[1152,4608]{1,0:T(8,128)(2,1)}), bf16[72,4608]{1,0:T(8,128)(2,1)}) %reduce-scatter.9.cloned.1.call-update) | async-done | bytes 663568 | tf_op jit(solution)/shard_map/reduce_scatter | solution.py:260
  903.0 124.4 %reduce-scatter.11.cloned.1.call-done = bf16[288,1152]{1,0:T(8,128)(2,1)} async-done(((bf16[4608,1152]{1,0:T(8,128)(2,1)}), bf16[288,1152]{1,0:T(8,128)(2,1)}) %reduce-scatter.11.cloned.1.call-update) | async-done | bytes 663568 | tf_op jit(solution)/shard_map/reduce_scatter | solution.py:203
  1027.5 73.0 %all-gather.1 = bf16[32,1,6912]{2,1,0:T(2,128)(2,1)S(1)} all-gather(bf16[1,1,6912]{2,1,0:T(2,128)(2,1)S(1)} %bitcast.158), channel_id=1, replica_groups=mesh['fsdp'=16,'dp'=2] {'fsdp','dp'}, dimensions={0}, use_global_device_ids=true | all-gather | bytes 456192 | tf_op jit(solution)/shard_map/all_gather | solution.py:252
  1104.3 2.1 convert_element_type.204
  (356 shorter events, 178.5 us)
Async XLA Ops:
  7.2 72.2 %copy-start = (bf16[72,6912]{1,0:T(8,128)(2,1)S(1)}, bf16[72,6912]{1,0:T(8,128)(2,1)}, u32[]{:S(2)}) copy-start(bf16[72,6912]{1,0:T(8,128)(2,1)} %param.21) | copy-start | bytes 2985988
  7.2 160.8 %all-reduce.18.cloned.1.call-start = ((), (), s32[]{:S(2)}) async-start(), calls=%async_computation.10 | async-start | bytes 884736
  81.4 2.8 copy-start.17
  81.4 5.3 copy-start.20
  81.4 5.6 copy-start.21
  81.4 5.8 copy-start.18
  81.4 63.9 %copy-start.2 = (bf16[1,256,1152]{2,1,0:T(8,128)(2,1)S(1)}, bf16[1,256,1152]{2,1,0:T(8,128)(2,1)}, u32[]{:S(2)}) copy-start(bf16[1,256,1152]{2,1,0:T(8,128)(2,1)} %param.18) | copy-start | bytes 1769476
  81.5 160.7 %all-gather.7.cloned.1.call-start = ((), (), s32[]{:S(2)}) async-start(), calls=%async_computation.4 | async-start | bytes 8460288 | tf_op jit(solution)/shard_map/all_gather | solution.py:157
  82.2 204.2 %all-gather.9.cloned.1.call-start = ((), (), s32[]{:S(2)}) async-start(), calls=%async_computation.5 | async-start | bytes 2820096 | tf_op jit(solution)/shard_map/all_gather | solution.py:159
  82.9 292.8 %all-gather.11.cloned.1.call-start = ((), (), s32[]{:S(2)}) async-start(), calls=%async_computation.6 | async-start | bytes 11280384 | tf_op jit(solution)/shard_map/all_gather | solution.py:181
  83.5 381.0 %all-gather.13.cloned.1.call-start = ((), (), s32[]{:S(2)}) async-start(), calls=%async_computation.7 | async-start | bytes 11280384 | tf_op jit(solution)/shard_map/all_gather | solution.py:183
  84.1 709.8 %reduce-scatter.15.cloned.1.call-start = ((), (), s32[]{:S(2)}) async-start(), calls=%async_computation.12 | async-start | bytes 2820096
  242.1 6.1 copy-start.19
  280.3 6.1 copy-start.15
  280.3 10.0 copy-start.3
  375.7 88.7 %copy-start.9 = (bf16[1,256,1152]{2,1,0:T(8,128)(2,1)S(1)}, bf16[1,256,1152]{2,1,0:T(8,128)(2,1)}, u32[]{:S(2)}) copy-start(bf16[1,256,1152]{2,1,0:T(8,128)(2,1)} %param.31) | copy-start | bytes 1769476
  472.7 8.3 copy-start.12
  472.7 8.5 copy-start.10
  481.0 1.3 copy-start.5
  482.8 1.1 copy-start.4
  486.4 307.5 %reduce-scatter.13.cloned.1.call-start = ((), (), s32[]{:S(2)}) async-start(), calls=%async_computation.11 | async-start | bytes 8460288
  679.3 223.7 %reduce-scatter.9.cloned.1.call-start = ((), (), s32[]{:S(2)}) async-start(), calls=%async_computation.8 | async-start | bytes 11280384 | tf_op jit(solution)/shard_map/reduce_scatter | solution.py:260
  689.0 338.4 %reduce-scatter.11.cloned.1.call-start = ((), (), s32[]{:S(2)}) async-start(), calls=%async_computation.9 | async-start | bytes 11280384 | tf_op jit(solution)/shard_map/reduce_scatter | solution.py:203
  700.7 2.0 copy-start.22
  700.7 403.6 %all-reduce.20.cloned.1.call-start = ((), (), s32[]{:S(2)}) async-start(), calls=%async_computation.13 | async-start | bytes 3981312 | tf_op jit(solution)/shard_map/psum | solution.py:291
  775.6 8.1 copy-start.11
  782.4 1.0 copy-start.6
  1100.5 2.5 copy-start.7
  1104.3 2.1 copy-start.16
  1104.3 2.9 copy-start.14
  1106.5 1.9 copy-start.13
  1107.2 2.3 copy-start.1
  (1 other events, 0.8 us)
Sparse Core Ops, SparseCore 0:
  81.6 86.3 all-reduce.17
  170.1 71.9 all-gather.6
  244.3 42.0 all-gather.8
  288.5 87.1 all-gather.10
  377.9 86.5 all-gather.12
  486.5 61.1 reduce-scatter.14
  679.4 99.2 reduce-scatter.12
  782.7 120.2 reduce-scatter.8
  907.1 120.3 reduce-scatter.10
  1029.8 72.9 all-reduce.19
